TPU v7x, 32 devices: a whole 2x2x4 slice. The times are simulated.
32 devices in a mesh: groups: 2 (over x), sample: 16 (over z, y, core).
Axes of the slice: x: 2, y: 2, z: 4, core: 2. Of those that a mesh axis runs over, the one named last changes fastest.
Arguments:
- prompt_states: bfloat16 [16384, 8192], P(('groups', 'sample')), parts along dimension 0, may hold values from -6 to 6
- page_table: int32 [128], P('groups'), parts along dimension 0, may hold values from 0 to 63, each once
- step_states: bfloat16 [2, 64, 8192], P(None, 'groups'), parts along dimension 1, may hold values from -15 to 15
- sample_order: int32 [64], P('groups'), parts along dimension 0, may hold values from 0 to 31, each once
- key_weight: bfloat16 [8192, 512], P('sample'), may hold values from -0.088388348 to 0.088388348
- value_weight: bfloat16 [8192, 512], P('sample'), may hold values from -0.0625 to 0.0625
- query_weight: bfloat16 [8192, 4096], P(None, 'sample'), may hold values from -0.121533978 to 0.121533978
- out_weight: bfloat16 [4096, 8192], P('sample'), may hold values from -0.125 to 0.125
Outputs:
- attn_out: bfloat16 [2, 64, 8192], P(None, 'groups', 'sample'), parts along dimension 1
There are 2 independent parts, one for each index of `groups`. A program takes and returns all parts, laid end to end along the dimension named above; an argument that names none is the same for every part. Nothing has to cross between parts.
Inputs may be any that keep to these rules, and one draw needn't show every extreme that they name: `page_table`: A permutation: entry p * 64 + j is the physical page that holds logical page j of prompt p; physical page r is rows r * 128 to (r + 1) * 128 - 1 of prompt_states. `sample_order`: A permutation; completion i continues prompt sample_order[i] // 32.
All inputs are finite; a program needn't handle non-finite values.
Results may differ from a plain program's by a relative error of at most 0.034.
Values may be sent and summed in bfloat16 or wider, within the bound.
A program may use at most 128 MiB of HBM per device.

v0:
```python
import jax
import jax.numpy as jnp
from jax import lax
from jax.sharding import PartitionSpec as P

D = 8192
HEAD_DIM = 128
KV_HEADS = 4
GQA = 8
PAGE = 128
PROMPT_PAGES = 64
rope_base = 1000000.0


def rotate(vector, position):
    half_dim = vector.shape[-1] // 2
    frequency = rope_base ** (-jnp.arange(half_dim, dtype=jnp.float32) * 2.0 / vector.shape[-1])
    angles = position.astype(jnp.float32)[..., None] * frequency
    cosine = jnp.cos(angles)
    sine_part = jnp.sin(angles)
    first_half = vector[..., :half_dim]
    second_half = vector[..., half_dim:]
    return jnp.concatenate(
        [
            first_half * cosine - second_half * sine_part,
            second_half * cosine + first_half * sine_part,
        ],
        axis=-1,
    )


def finish_heads(prefix_top, prefix_total, prefix_sum, queries, new_keys, new_values):
    score_scale = queries.shape[-1] ** (-0.5)
    query_wide = queries.astype(jnp.float32)
    key_wide = new_keys.astype(jnp.float32)
    value_wide = new_values.astype(jnp.float32)
    own_score = jnp.sum(query_wide * key_wide, axis=-1) * score_scale
    back_score = jnp.sum(query_wide[1] * key_wide[0], axis=-1) * score_scale
    first_high = jnp.maximum(prefix_top[0], own_score[0])
    first_old = jnp.exp(prefix_top[0] - first_high)
    first_own = jnp.exp(own_score[0] - first_high)
    first_out = (first_old[..., None] * prefix_sum[0] + first_own[..., None] * value_wide[0]) / (
        first_old * prefix_total[0] + first_own
    )[..., None]
    second_high = jnp.maximum(jnp.maximum(prefix_top[1], own_score[1]), back_score)
    second_old = jnp.exp(prefix_top[1] - second_high)
    second_back = jnp.exp(back_score - second_high)
    second_own = jnp.exp(own_score[1] - second_high)
    second_num = (
        second_old[..., None] * prefix_sum[1]
        + second_back[..., None] * value_wide[0]
        + second_own[..., None] * value_wide[1]
    )
    second_out = second_num / (second_old * prefix_total[1] + second_back + second_own)[..., None]
    return jnp.stack([first_out, second_out]).astype(jnp.bfloat16)


def on_device(
    prompt_states,
    page_table,
    step_states,
    sample_order,
    key_weight,
    value_weight,
    query_weight,
    out_weight,
):
    devices = lax.axis_size("sample")
    own_index = lax.axis_index("sample")
    row_count = prompt_states.shape[0]
    pages_here = row_count // PAGE
    heads_here = query_weight.shape[1] // HEAD_DIM
    total_pages = page_table.shape[0]
    prompts = total_pages // PROMPT_PAGES
    samples = sample_order.shape[0]
    group_size = samples // prompts
    score_scale = HEAD_DIM ** (-0.5)
    own_kv = own_index * heads_here // GQA
    slot_of = (
        jnp.zeros((total_pages,), jnp.int32)
        .at[page_table]
        .set(jnp.arange(total_pages, dtype=jnp.int32))
    )
    local_slots = lax.dynamic_slice_in_dim(slot_of, own_index * pages_here, pages_here)
    positions = (local_slots % PROMPT_PAGES * PAGE)[:, None] + jnp.arange(PAGE, dtype=jnp.int32)[
        None, :
    ]
    positions = positions.reshape(row_count)
    wide_states = step_states.reshape(2 * samples, D)
    key_piece = lax.all_gather(key_weight, "sample", axis=0, tiled=True)
    value_piece = lax.all_gather(value_weight, "sample", axis=0, tiled=True)
    piece_rows = key_piece.shape[0]
    key_acc = jnp.einsum(
        "rn,nkd->krd",
        prompt_states,
        key_piece.reshape(piece_rows, KV_HEADS, HEAD_DIM),
        preferred_element_type=jnp.float32,
    )
    value_acc = jnp.einsum(
        "rn,nkd->krd",
        prompt_states,
        value_piece.reshape(piece_rows, KV_HEADS, HEAD_DIM),
        preferred_element_type=jnp.float32,
    )
    key_head = lax.dynamic_slice_in_dim(key_piece, own_kv * HEAD_DIM, HEAD_DIM, 1)
    value_head = lax.dynamic_slice_in_dim(value_piece, own_kv * HEAD_DIM, HEAD_DIM, 1)
    key_step = jnp.dot(wide_states, key_head, preferred_element_type=jnp.float32)
    value_step = jnp.dot(wide_states, value_head, preferred_element_type=jnp.float32)
    key_acc, value_acc, key_step, value_step = (key_acc, value_acc, key_step, value_step)
    page_keys = rotate(key_acc, positions[None, :]).astype(jnp.bfloat16)
    page_values = value_acc.astype(jnp.bfloat16)
    step_place = (PROMPT_PAGES * PAGE + jnp.arange(2, dtype=jnp.int32))[:, None, None]
    queries = jnp.dot(wide_states, query_weight, preferred_element_type=jnp.float32).reshape(
        2, samples, heads_here, HEAD_DIM
    )
    queries = rotate(queries, step_place).astype(jnp.bfloat16)
    new_keys = rotate(key_step.reshape(2, samples, HEAD_DIM), step_place[:, :, 0]).astype(
        jnp.bfloat16
    )
    new_values = value_step.reshape(2, samples, HEAD_DIM).astype(jnp.bfloat16)
    inverse = (
        jnp.zeros((samples,), jnp.int32).at[sample_order].set(jnp.arange(samples, dtype=jnp.int32))
    )
    spread = devices // KV_HEADS
    send_keys = jnp.repeat(page_keys, spread, axis=0)
    send_values = jnp.repeat(page_values, spread, axis=0)
    all_keys, all_values = (
        lax.all_to_all(send_keys, "sample", split_axis=0, concat_axis=1, tiled=True),
        lax.all_to_all(send_values, "sample", split_axis=0, concat_axis=1, tiled=True),
    )
    logical = page_table.reshape(prompts, PROMPT_PAGES)
    all_keys = all_keys.reshape(total_pages, PAGE, HEAD_DIM)[logical].reshape(
        prompts, PROMPT_PAGES * PAGE, HEAD_DIM
    )
    all_values = all_values.reshape(total_pages, PAGE, HEAD_DIM)[logical].reshape(
        prompts, PROMPT_PAGES * PAGE, HEAD_DIM
    )
    sorted_query = queries[:, inverse].reshape(2, prompts, group_size, heads_here, HEAD_DIM)
    scores = (
        jnp.einsum("spmhd,pld->spmhl", sorted_query, all_keys, preferred_element_type=jnp.float32)
        * score_scale
    )
    prefix_top = jnp.max(scores, axis=-1)
    weights = jnp.exp(scores - prefix_top[..., None])
    prefix_total = jnp.sum(weights, axis=-1)
    prefix_sum = jnp.einsum(
        "spmhl,pld->spmhd",
        weights.astype(jnp.bfloat16),
        all_values,
        preferred_element_type=jnp.float32,
    )
    prefix_top = prefix_top.reshape(2, samples, heads_here)[:, sample_order]
    prefix_total = prefix_total.reshape(2, samples, heads_here)[:, sample_order]
    prefix_sum = prefix_sum.reshape(2, samples, heads_here, HEAD_DIM)[:, sample_order]
    head_out = finish_heads(
        prefix_top,
        prefix_total,
        prefix_sum,
        queries,
        new_keys[:, :, None, :],
        new_values[:, :, None, :],
    )
    flat_heads = head_out.reshape(2, samples, heads_here * HEAD_DIM)
    head_terms = jnp.einsum(
        "srk,kd->srd", flat_heads, out_weight, preferred_element_type=jnp.float32
    )
    return lax.psum_scatter(
        head_terms.astype(jnp.bfloat16), "sample", scatter_dimension=2, tiled=True
    )


def solution(mesh):
    in_specs = (
        P(("groups", "sample"), None),
        P("groups"),
        P(None, "groups", None),
        P("groups"),
        P("sample", None),
        P("sample", None),
        P(None, "sample"),
        P("sample", None),
    )
    out_specs = P(None, "groups", "sample")
    return jax.shard_map(
        on_device, mesh=mesh, in_specs=in_specs, out_specs=out_specs, check_vma=False
    )
```

profile of v0, /device:TPU:0, one launch (start us, length us, event | category | flops | bytes accessed | tf_op | source)
XLA Modules:
  0.0 351.2 jit_solution(6273337491218514646)
XLA Ops:
  10.2 77.0 %all-gather.3.cloned.1.call-done = bf16[8192,512]{1,0:T(8,128)(2,1)} async-done(((bf16[512,512]{1,0:T(8,128)(2,1)}), bf16[8192,512]{1,0:T(8,128)(2,1)}) %all-gather.3.cloned.1.call-update) | async-done | bytes 8388624 | tf_op jit(solution)/shard_map/all_gather | solution.py:90
  87.2 11.5 %copy.36 = bf16[8192,512]{0,1:T(8,128)(2,1)} copy(bf16[8192,512]{1,0:T(8,128)(2,1)} %all-gather.3.cloned.1.call-done) | data formatting | bytes 16777216 | tf_op jit(solution)/shard_map/all_gather | solution.py:90
  98.6 9.5 %fusion.16 = f32[4,512,128]{1,2,0:T(8,128)S(1)} fusion(bf16[8192,4,128]{0,2,1:T(8,128)(2,1)} %bitcast.153, bf16[512,8192]{1,0:T(8,128)(2,1)} %param.8), kind=kOutput, calls=%fused_computation.26 | convolution fusion | flops 4294967296 | bytes 17825792 | tf_op jit(solution)/shard_map/rn,nkd->krd/dot_general | solution.py:93
  108.7 1.8 broadcast_in_dim.13
  110.5 3.7 %all-to-all-start = ((bf16[16,512,128]{2,1,0:T(8,128)(2,1)}), bf16[16,512,128]{2,1,0:T(8,128)(2,1)S(1)}, u32[]{:S(2)}, u32[]{:S(2)}) async-start(bf16[16,512,128]{2,1,0:T(8,128)(2,1)} %bitcast.4), calls=%async_computation | async-start | bytes 4194304 | tf_op jit(solution)/shard_map/all_to_all | solution.py:128
  114.2 6.4 %copy.61 = bf16[256,8192]{1,0:T(8,128)(2,1)} copy(bf16[256,8192]{0,1:T(8,128)(2,1)} %bitcast.158) | data formatting | bytes 8388608 | tf_op jit(solution)/shard_map/dot_general | solution.py:113
  120.7 4.3 %fusion.37 = f32[2,32,2,128]{3,1,2,0:T(8,128)S(1)} fusion(bf16[2,128,8192,1]{2,1,0,3:T(8,128)(2,1)} %bitcast.152, bf16[2,32,8192]{2,1,0:T(8,128)(2,1)S(1)} %copy-done), kind=kOutput, calls=%fused_computation.33 | convolution fusion | flops 268435456 | bytes 5308416 | tf_op jit(solution)/shard_map/dot_general | solution.py:113
  125.1 69.1 %all-gather.5.cloned.1.call-done = bf16[8192,512]{1,0:T(8,128)(2,1)} async-done(((bf16[512,512]{1,0:T(8,128)(2,1)}), bf16[8192,512]{1,0:T(8,128)(2,1)}) %all-gather.5.cloned.1.call-update) | async-done | bytes 8388624 | tf_op jit(solution)/shard_map/all_gather | solution.py:91
  194.2 11.4 %copy.44 = bf16[8192,512]{0,1:T(8,128)(2,1)} copy(bf16[8192,512]{1,0:T(8,128)(2,1)} %all-gather.5.cloned.1.call-done) | data formatting | bytes 16777216 | tf_op jit(solution)/shard_map/all_gather | solution.py:91
  205.6 11.1 %fusion.22 = bf16[4,512,128]{1,2,0:T(8,128)(2,1)} fusion(bf16[8192,4,128]{0,2,1:T(8,128)(2,1)} %bitcast.154, bf16[512,8192]{1,0:T(8,128)(2,1)} %param.8), kind=kOutput, calls=%fused_computation.28 | convolution fusion | flops 4295229440 | bytes 17301504 | tf_op jit(solution)/shard_map/rn,nkd->krd/dot_general | solution.py:99
  216.7 2.1 copy.45
  218.7 2.8 broadcast_in_dim.17
  221.6 7.3 %all-to-all-start.1 = ((bf16[16,512,128]{2,1,0:T(8,128)(2,1)}), bf16[16,512,128]{2,1,0:T(8,128)(2,1)}, u32[]{:S(2)}, u32[]{:S(2)}) async-start(bf16[16,512,128]{2,1,0:T(8,128)(2,1)} %bitcast.26), calls=%async_computation.1 | async-start | bytes 4194304 | tf_op jit(solution)/shard_map/all_to_all | solution.py:129
  229.2 0.9 scatter_custom_fusion.1
  230.7 2.1 fusion.14
  233.3 2.1 fusion.34
  235.4 2.1 gather_fusion
  237.5 4.2 %fusion.77 = (f32[2,32,2]{1,2,0:T(2,128)S(1)}, f32[2,1,32,2,8192]{4,2,3,0,1:T(8,128)}) fusion(bf16[8192,128,1,1]{1,0,3,2:T(8,128)(2,1)} %bitcast.156, bf16[2,32,2,128]{3,2,0,1:T(2,128)(2,1)S(1)} %bitcast.163), kind=kOutput, calls=%fused_computation.111 | convolution fusion | flops 270532480 | bytes 6324736 | tf_op jit(solution)/shard_map/spmhd,pld->spmhl/dot_general | solution.py:140
  241.9 2.9 fusion.6
  247.1 22.9 %all-to-all-done.1 = bf16[16,512,128]{2,1,0:T(8,128)(2,1)} async-done(((bf16[16,512,128]{2,1,0:T(8,128)(2,1)}), bf16[16,512,128]{2,1,0:T(8,128)(2,1)}, u32[]{:S(2)}, u32[]{:S(2)}) %all-to-all-start.1) | async-done | bytes 2097184 | tf_op jit(solution)/shard_map/all_to_all | solution.py:129
  270.0 2.5 gather_fusion.3
  272.6 3.0 fusion.25
  276.7 4.0 %convolution_convert_fusion = bf16[2,32,8192]{2,1,0:T(8,128)(2,1)} fusion(bf16[256,8192]{1,0:T(8,128)(2,1)} %param.15, bf16[1,32,256]{2,1,0:T(8,128)(2,1)S(1)} %stack.10, bf16[1,32,256]{2,1,0:T(8,128)(2,1)S(1)} %stack.9), kind=kOutput, calls=%fused_computation.10 | convolution fusion | flops 268976128 | bytes 5275648 | tf_op jit(solution)/shard_map/srk,kd->srd/dot_general | solution.py:164
  280.7 64.0 %reduce-scatter.2.cloned.1.call-done = bf16[2,32,512]{2,1,0:T(8,128)(2,1)} async-done(((bf16[2,32,8192]{2,1,0:T(8,128)(2,1)}), bf16[2,32,512]{2,1,0:T(8,128)(2,1)}) %reduce-scatter.2.cloned.1.call-update) | async-done | bytes 65552 | tf_op jit(solution)/shard_map/reduce_scatter | solution.py:167
  (63 shorter events, 9.0 us)
Async XLA Ops:
  6.5 114.2 %copy-start = (bf16[2,32,8192]{2,1,0:T(8,128)(2,1)S(1)}, bf16[2,32,8192]{2,1,0:T(8,128)(2,1)}, u32[]{:S(2)}) copy-start(bf16[2,32,8192]{2,1,0:T(8,128)(2,1)} %param.10) | copy-start | bytes 3145732
  6.5 80.6 %all-gather.3.cloned.1.call-start = ((), (), s32[]{:S(2)}) async-start(), calls=%async_computation.3 | async-start | bytes 8912896 | tf_op jit(solution)/shard_map/all_gather | solution.py:90
  7.3 186.9 %all-gather.5.cloned.1.call-start = ((), (), s32[]{:S(2)}) async-start(), calls=%async_computation.4 | async-start | bytes 8912896 | tf_op jit(solution)/shard_map/all_gather | solution.py:91
  110.5 108.3 %all-to-all-start = ((bf16[16,512,128]{2,1,0:T(8,128)(2,1)}), bf16[16,512,128]{2,1,0:T(8,128)(2,1)S(1)}, u32[]{:S(2)}, u32[]{:S(2)}) async-start(bf16[16,512,128]{2,1,0:T(8,128)(2,1)} %bitcast.4), calls=%async_computation | async-start | bytes 4194304 | tf_op jit(solution)/shard_map/all_to_all | solution.py:128
  216.7 12.5 %copy-start.1 = (s32[32]{0:T(128)S(1)}, s32[32]{0:T(128)}, u32[]{:S(2)}) copy-start(s32[32]{0:T(128)} %param.11) | copy-start | bytes 388
  221.6 48.4 %all-to-all-start.1 = ((bf16[16,512,128]{2,1,0:T(8,128)(2,1)}), bf16[16,512,128]{2,1,0:T(8,128)(2,1)}, u32[]{:S(2)}, u32[]{:S(2)}) async-start(bf16[16,512,128]{2,1,0:T(8,128)(2,1)} %bitcast.26), calls=%async_computation.1 | async-start | bytes 4194304 | tf_op jit(solution)/shard_map/all_to_all | solution.py:129
  228.9 115.8 %reduce-scatter.2.cloned.1.call-start = ((), (), s32[]{:S(2)}) async-start(), calls=%async_computation.5 | async-start | bytes 1114112 | tf_op jit(solution)/shard_map/reduce_scatter | solution.py:167
Sparse Core Ops, SparseCore 0:
  9.5 77.5 all-gather.2
  89.3 104.7 all-gather.4
  280.8 63.8 reduce-scatter.1
where the time goes:
time: 352 us; the launch traced here: 351 us
  waiting for transfers between devices  234 us (66%)
  local copies, waits for them, and re-layouts  46.4 us (13%)
  matrix products  40.4 us (11%)
  between operations  13.4 us (4%)
  starting transfers between devices  11.1 us (3%)
  other arithmetic  5.57 us (2%)
    all_gather x1, waiting for transfers between devices, on_device(): key_piece = lax.all_gather(key_weight, 'sample', axis=0, tiled=True)  77 us
    all_gather x1, waiting for transfers between devices, on_device(): value_piece = lax.all_gather(value_weight, 'sample', axis=0, tiled=True)  69.1 us
    reduce_scatter x1, waiting for transfers between devices, on_device(): lax.psum_scatter(head_terms.astype(jnp.bfloat16), 'sample', scatter_dimen...  64 us
    all_to_all x1, waiting for transfers between devices, on_device(): lax.all_to_all(send_values, 'sample', split_axis=0, concat_axis=1, tiled=...  22.9 us
    all_gather x1, local copies, waits for them, and re-layouts, on_device(): key_piece = lax.all_gather(key_weight, 'sample', axis=0, tiled=True)  11.5 us
    all_gather x1, local copies, waits for them, and re-layouts, on_device(): value_piece = lax.all_gather(value_weight, 'sample', axis=0, tiled=True)  11.4 us
    dot_general x1, matrix products, on_device(): jnp.einsum('rn,nkd->krd', prompt_states, value_piece.reshape(piece_rows,...  11.1 us
    dot_general x1, matrix products, on_device(): jnp.einsum('rn,nkd->krd', prompt_states, key_piece.reshape(piece_rows, KV...  9.54 us
  transfers between devices with their start and end apart: 5, of which 4 were waited for; matrix products, arithmetic and copies ran while one was open for 22% of the time, Pallas kernels for 0%

commit v1 on v0

--- a/solution.py
+++ b/solution.py
@@ -10,6 +10,19 @@
 PAGE = 128
 PROMPT_PAGES = 64
 rope_base = 1000000.0
+
+
+def digits_choose(buf, mesh_ax):
+    dev_n = lax.axis_size(mesh_ax)
+    part_now = [(k - 1, k) for k in range(1, dev_n)] + [(dev_n - 1, 0)]
+    left_arr = buf
+    bank = [left_arr]
+    for _ in range(dev_n - 1):
+        left_arr = lax.ppermute(left_arr, mesh_ax, part_now)
+        bank += [left_arr]
+    back = jnp.concatenate([*reversed(bank)], 0)
+    built = jnp.roll(back, (lax.axis_index(mesh_ax) + 1) * left_arr.shape[0], 0)
+    return built
 
 
 def rotate(vector, position):
@@ -88,7 +101,7 @@
     positions = positions.reshape(row_count)
     wide_states = step_states.reshape(2 * samples, D)
     key_piece = lax.all_gather(key_weight, "sample", axis=0, tiled=True)
-    value_piece = lax.all_gather(value_weight, "sample", axis=0, tiled=True)
+    value_piece = digits_choose(value_weight, "sample")
     piece_rows = key_piece.shape[0]
     key_acc = jnp.einsum(
         "rn,nkd->krd",

time: 352 us -> 481 us (1.37)
  waiting for transfers between devices: 234 us -> 299 us
  local copies, waits for them, and re-layouts: 46.4 us -> 105 us
    ppermute x0 -> x15, waiting for transfers between devices: none -> 198 us  [digits_choose(): left_arr = lax.ppermute(left_arr, mesh_ax, part_now)]
    all_gather x1, waiting for transfers between devices: 77 us -> 0.02 us  [on_device(): key_piece = lax.all_gather(key_weight, 'sample', axis=0, tiled=True)]
    all_gather x1 -> x0, waiting for transfers between devices: 69.1 us -> none  [on_device(): value_piece = lax.all_gather(value_weight, 'sample', axis=0, tiled=True)]
    unnamed x4 -> x79, local copies, waits for them, and re-layouts: 0.01 us -> 49.7 us
    all_to_all x1, waiting for transfers between devices: 0.01 us -> 20.7 us  [on_device(): lax.all_to_all(send_keys, 'sample', split_axis=0, concat_axis=1, tiled=True)]
    dynamic_slice x0 -> x2, local copies, waits for them, and re-layouts: none -> 18.9 us  [digits_choose(): built = jnp.roll(back, (lax.axis_index(mesh_ax) + 1) * left_arr.shape[0], 0)]
    all_gather x1 -> x0, local copies, waits for them, and re-layouts: 11.4 us -> none  [on_device(): value_piece = lax.all_gather(value_weight, 'sample', axis=0, tiled=True)]
    all_to_all x1, waiting for transfers between devices: 22.9 us -> 14.6 us  [on_device(): lax.all_to_all(send_values, 'sample', split_axis=0, concat_axis=1, tiled=...]
  transfers between devices with their start and end apart: 5 -> 19, of which waited for: 4 -> 18; matrix products, arithmetic and copies ran while one was open for 22% -> 25% of each run, Pallas kernels for 0% -> 0%
where the time goes in v1:
time: 481 us; the launch traced here: 479 us
  waiting for transfers between devices  299 us (62%)
  local copies, waits for them, and re-layouts  105 us (22%)
  matrix products  39.5 us (8%)
  starting transfers between devices  15.5 us (3%)
  between operations  13.8 us (3%)
  other arithmetic  5.74 us (1%)
    ppermute x15, waiting for transfers between devices, digits_choose(): left_arr = lax.ppermute(left_arr, mesh_ax, part_now)  198 us
    reduce_scatter x1, waiting for transfers between devices, on_device(): lax.psum_scatter(head_terms.astype(jnp.bfloat16), 'sample', scatter_dimen...  65.5 us
    unnamed x79, local copies, waits for them, and re-layouts  49.7 us
    all_to_all x1, waiting for transfers between devices, on_device(): lax.all_to_all(send_keys, 'sample', split_axis=0, concat_axis=1, tiled=True)  20.7 us
    dynamic_slice x2, local copies, waits for them, and re-layouts, digits_choose(): built = jnp.roll(back, (lax.axis_index(mesh_ax) + 1) * left_arr.shape[0], 0)  18.9 us
    all_to_all x1, waiting for transfers between devices, on_device(): lax.all_to_all(send_values, 'sample', split_axis=0, concat_axis=1, tiled=...  14.6 us
    all_gather x1, local copies, waits for them, and re-layouts, on_device(): key_piece = lax.all_gather(key_weight, 'sample', axis=0, tiled=True)  12 us
    all_to_all x1, starting transfers between devices, on_device(): lax.all_to_all(send_keys, 'sample', split_axis=0, concat_axis=1, tiled=True)  11.2 us
  transfers between devices with their start and end apart: 19, of which 18 were waited for; matrix products, arithmetic and copies ran while one was open for 25% of the time, Pallas kernels for 0%

profile of v1, /device:TPU:0, one launch (start us, length us, event | category | flops | bytes accessed | tf_op | source)
XLA Modules:
  0.0 478.6 jit_solution(3470243943868632162)
XLA Ops:
  7.0 12.1 %collective-permute-done = bf16[512,512]{1,0:T(8,128)(2,1)S(1)} collective-permute-done((bf16[512,512]{1,0:T(8,128)(2,1)}, bf16[512,512]{1,0:T(8,128)(2,1)S(1)}, u32[]{:S(2)}, u32[]{:S(2)}) %collective-permute-start) | collective-permute-done | bytes 524320 | tf_op jit(solution)/shard_map/ppermute | solution.py:21
  19.1 11.3 %collective-permute-done.1 = bf16[512,512]{1,0:T(8,128)(2,1)S(1)} collective-permute-done((bf16[512,512]{1,0:T(8,128)(2,1)S(1)}, bf16[512,512]{1,0:T(8,128)(2,1)S(1)}, u32[]{:S(2)}, u32[]{:S(2)}) %collective-permute-start.1) | collective-permute-done | bytes 524320 | tf_op jit(solution)/shard_map/ppermute | solution.py:21
  30.4 22.4 %collective-permute-done.2 = bf16[512,512]{1,0:T(8,128)(2,1)S(1)} collective-permute-done((bf16[512,512]{1,0:T(8,128)(2,1)S(1)}, bf16[512,512]{1,0:T(8,128)(2,1)S(1)}, u32[]{:S(2)}, u32[]{:S(2)}) %collective-permute-start.2) | collective-permute-done | bytes 524320 | tf_op jit(solution)/shard_map/ppermute | solution.py:21
  52.8 11.5 %collective-permute-done.3 = bf16[512,512]{1,0:T(8,128)(2,1)S(1)} collective-permute-done((bf16[512,512]{1,0:T(8,128)(2,1)S(1)}, bf16[512,512]{1,0:T(8,128)(2,1)S(1)}, u32[]{:S(2)}, u32[]{:S(2)}) %collective-permute-start.3) | collective-permute-done | bytes 524320 | tf_op jit(solution)/shard_map/ppermute | solution.py:21
  65.1 22.5 %collective-permute-done.4 = bf16[512,512]{1,0:T(8,128)(2,1)S(1)} collective-permute-done((bf16[512,512]{1,0:T(8,128)(2,1)S(1)}, bf16[512,512]{1,0:T(8,128)(2,1)S(1)}, u32[]{:S(2)}, u32[]{:S(2)}) %collective-permute-start.4) | collective-permute-done | bytes 524320 | tf_op jit(solution)/shard_map/ppermute | solution.py:21
  88.4 16.1 %collective-permute-done.5 = bf16[512,512]{1,0:T(8,128)(2,1)S(1)} collective-permute-done((bf16[512,512]{1,0:T(8,128)(2,1)S(1)}, bf16[512,512]{1,0:T(8,128)(2,1)S(1)}, u32[]{:S(2)}, u32[]{:S(2)}) %collective-permute-start.5) | collective-permute-done | bytes 524320 | tf_op jit(solution)/shard_map/ppermute | solution.py:21
  105.3 11.4 %collective-permute-done.6 = bf16[512,512]{1,0:T(8,128)(2,1)S(1)} collective-permute-done((bf16[512,512]{1,0:T(8,128)(2,1)S(1)}, bf16[512,512]{1,0:T(8,128)(2,1)S(1)}, u32[]{:S(2)}, u32[]{:S(2)}) %collective-permute-start.6) | collective-permute-done | bytes 524320 | tf_op jit(solution)/shard_map/ppermute | solution.py:21
  117.5 11.3 %collective-permute-done.7 = bf16[512,512]{1,0:T(8,128)(2,1)S(1)} collective-permute-done((bf16[512,512]{1,0:T(8,128)(2,1)S(1)}, bf16[512,512]{1,0:T(8,128)(2,1)S(1)}, u32[]{:S(2)}, u32[]{:S(2)}) %collective-permute-start.7) | collective-permute-done | bytes 524320 | tf_op jit(solution)/shard_map/ppermute | solution.py:21
  129.6 11.3 %collective-permute-done.8 = bf16[512,512]{1,0:T(8,128)(2,1)S(1)} collective-permute-done((bf16[512,512]{1,0:T(8,128)(2,1)S(1)}, bf16[512,512]{1,0:T(8,128)(2,1)S(1)}, u32[]{:S(2)}, u32[]{:S(2)}) %collective-permute-start.8) | collective-permute-done | bytes 524320 | tf_op jit(solution)/shard_map/ppermute | solution.py:21
  141.7 11.3 %collective-permute-done.9 = bf16[512,512]{1,0:T(8,128)(2,1)S(1)} collective-permute-done((bf16[512,512]{1,0:T(8,128)(2,1)S(1)}, bf16[512,512]{1,0:T(8,128)(2,1)S(1)}, u32[]{:S(2)}, u32[]{:S(2)}) %collective-permute-start.9) | collective-permute-done | bytes 524320 | tf_op jit(solution)/shard_map/ppermute | solution.py:21
  153.8 11.3 %collective-permute-done.10 = bf16[512,512]{1,0:T(8,128)(2,1)S(1)} collective-permute-done((bf16[512,512]{1,0:T(8,128)(2,1)S(1)}, bf16[512,512]{1,0:T(8,128)(2,1)S(1)}, u32[]{:S(2)}, u32[]{:S(2)}) %collective-permute-start.10) | collective-permute-done | bytes 524320 | tf_op jit(solution)/shard_map/ppermute | solution.py:21
  165.9 11.3 %collective-permute-done.11 = bf16[512,512]{1,0:T(8,128)(2,1)S(1)} collective-permute-done((bf16[512,512]{1,0:T(8,128)(2,1)S(1)}, bf16[512,512]{1,0:T(8,128)(2,1)S(1)}, u32[]{:S(2)}, u32[]{:S(2)}) %collective-permute-start.11) | collective-permute-done | bytes 524320 | tf_op jit(solution)/shard_map/ppermute | solution.py:21
  178.1 11.3 %collective-permute-done.12 = bf16[512,512]{1,0:T(8,128)(2,1)S(1)} collective-permute-done((bf16[512,512]{1,0:T(8,128)(2,1)S(1)}, bf16[512,512]{1,0:T(8,128)(2,1)S(1)}, u32[]{:S(2)}, u32[]{:S(2)}) %collective-permute-start.12) | collective-permute-done | bytes 524320 | tf_op jit(solution)/shard_map/ppermute | solution.py:21
  190.2 11.4 %collective-permute-done.13 = bf16[512,512]{1,0:T(8,128)(2,1)} collective-permute-done((bf16[512,512]{1,0:T(8,128)(2,1)S(1)}, bf16[512,512]{1,0:T(8,128)(2,1)}, u32[]{:S(2)}, u32[]{:S(2)}) %collective-permute-start.13) | collective-permute-done | bytes 524320 | tf_op jit(solution)/shard_map/ppermute | solution.py:21
  201.7 11.5 %collective-permute-done.14 = bf16[512,512]{1,0:T(8,128)(2,1)} collective-permute-done((bf16[512,512]{1,0:T(8,128)(2,1)}, bf16[512,512]{1,0:T(8,128)(2,1)}, u32[]{:S(2)}, u32[]{:S(2)}) %collective-permute-start.14) | collective-permute-done | bytes 524320 | tf_op jit(solution)/shard_map/ppermute | solution.py:21
  255.7 7.2 %constant_dynamic-slice_fusion = bf16[8192,512]{1,0:T(8,128)(2,1)} fusion(bf16[16384,512]{1,0:T(8,128)(2,1)} %constant_dynamic-update-slice_fusion, s32[]{:T(128)S(6)} %select_n.57), kind=kLoop, calls=%fused_computation.132 | loop fusion | bytes 16777220 | tf_op jit(solution)/shard_map/jit(_roll_dynamic)/dynamic_slice | solution.py:24
  262.9 11.7 %copy.44 = bf16[8192,512]{0,1:T(8,128)(2,1)} copy(bf16[8192,512]{1,0:T(8,128)(2,1)} %constant_dynamic-slice_fusion) | data formatting | bytes 16777216 | tf_op jit(solution)/shard_map/jit(_roll_dynamic)/dynamic_slice | solution.py:24
  274.6 10.3 %fusion.22 = bf16[4,512,128]{1,2,0:T(8,128)(2,1)S(1)} fusion(bf16[8192,4,128]{0,2,1:T(8,128)(2,1)} %bitcast.153, bf16[512,8192]{1,0:T(8,128)(2,1)} %param.8), kind=kOutput, calls=%fused_computation.28 | convolution fusion | flops 4295229440 | bytes 17301504 | tf_op jit(solution)/shard_map/rn,nkd->krd/dot_general | solution.py:112
  292.4 12.0 %copy.36 = bf16[8192,512]{0,1:T(8,128)(2,1)} copy(bf16[8192,512]{1,0:T(8,128)(2,1)} %all-gather.2.cloned.1.call-done) | data formatting | bytes 16777216 | tf_op jit(solution)/shard_map/all_gather | solution.py:103
  304.4 9.5 %fusion.16 = f32[4,512,128]{1,2,0:T(8,128)S(1)} fusion(bf16[8192,4,128]{0,2,1:T(8,128)(2,1)} %bitcast.154, bf16[512,8192]{1,0:T(8,128)(2,1)} %param.8), kind=kOutput, calls=%fused_computation.26 | convolution fusion | flops 4294967296 | bytes 17825792 | tf_op jit(solution)/shard_map/rn,nkd->krd/dot_general | solution.py:106
  317.1 14.6 %all-to-all-done.1 = bf16[16,512,128]{2,1,0:T(8,128)(2,1)S(1)} async-done(((bf16[16,512,128]{2,1,0:T(8,128)(2,1)}), bf16[16,512,128]{2,1,0:T(8,128)(2,1)S(1)}, u32[]{:S(2)}, u32[]{:S(2)}) %all-to-all-start.1) | async-done | bytes 2097184 | tf_op jit(solution)/shard_map/all_to_all | solution.py:142
  334.5 11.2 %all-to-all-start = ((bf16[16,512,128]{2,1,0:T(8,128)(2,1)}), bf16[16,512,128]{2,1,0:T(8,128)(2,1)}, u32[]{:S(2)}, u32[]{:S(2)}) async-start(bf16[16,512,128]{2,1,0:T(8,128)(2,1)} %bitcast.4), calls=%async_computation | async-start | bytes 4194304 | tf_op jit(solution)/shard_map/all_to_all | solution.py:141
  366.2 20.7 %all-to-all-done = bf16[16,512,128]{2,1,0:T(8,128)(2,1)} async-done(((bf16[16,512,128]{2,1,0:T(8,128)(2,1)}), bf16[16,512,128]{2,1,0:T(8,128)(2,1)}, u32[]{:S(2)}, u32[]{:S(2)}) %all-to-all-start) | async-done | bytes 2097184 | tf_op jit(solution)/shard_map/all_to_all | solution.py:141
  406.3 65.5 %reduce-scatter.2.cloned.1.call-done = bf16[2,32,512]{2,1,0:T(8,128)(2,1)} async-done(((bf16[2,32,8192]{2,1,0:T(8,128)(2,1)}), bf16[2,32,512]{2,1,0:T(8,128)(2,1)}) %reduce-scatter.2.cloned.1.call-update) | async-done | bytes 65552 | tf_op jit(solution)/shard_map/reduce_scatter | solution.py:180
  (166 shorter events, 104.0 us)
Async XLA Ops:
  6.5 345.8 %copy-start = (bf16[2,32,8192]{2,1,0:T(8,128)(2,1)S(1)}, bf16[2,32,8192]{2,1,0:T(8,128)(2,1)}, u32[]{:S(2)}) copy-start(bf16[2,32,8192]{2,1,0:T(8,128)(2,1)} %param.10) | copy-start | bytes 3145732
  6.5 248.3 %copy-start.1 = (bf16[512,512]{1,0:T(8,128)(2,1)S(1)}, bf16[512,512]{1,0:T(8,128)(2,1)}, u32[]{:S(2)}) copy-start(bf16[512,512]{1,0:T(8,128)(2,1)} %param.13) | copy-start | bytes 1572868
  6.5 285.8 %all-gather.2.cloned.1.call-start = ((), (), s32[]{:S(2)}) async-start(), calls=%async_computation.3 | async-start | bytes 8912896 | tf_op jit(solution)/shard_map/all_gather | solution.py:103
  6.5 12.5 %collective-permute-start = (bf16[512,512]{1,0:T(8,128)(2,1)}, bf16[512,512]{1,0:T(8,128)(2,1)S(1)}, u32[]{:S(2)}, u32[]{:S(2)}) collective-permute-start(bf16[512,512]{1,0:T(8,128)(2,1)} %param.13), channel_id=1, source_target_pairs={{0,1},{1,2},{2,3},{3,4},{4,5},{5,6},{6,7},{7,8},{8,9},{9,10},{10,1... | collective-permute-start | bytes 1572872 | tf_op jit(solution)/shard_map/ppermute | solution.py:21
  19.1 11.3 %collective-permute-start.1 = (bf16[512,512]{1,0:T(8,128)(2,1)S(1)}, bf16[512,512]{1,0:T(8,128)(2,1)S(1)}, u32[]{:S(2)}, u32[]{:S(2)}) collective-permute-start(bf16[512,512]{1,0:T(8,128)(2,1)S(1)} %collective-permute-done), channel_id=1, source_target_pairs={{0,1},{1,2},{2,3},{3,4},{4,5},{5,6},{6,7},{7,8},{8,9},{9,10},{10,1... | collective-permute-start | bytes 1572872 | tf_op jit(solution)/shard_map/ppermute | solution.py:21
  30.4 22.4 %collective-permute-start.2 = (bf16[512,512]{1,0:T(8,128)(2,1)S(1)}, bf16[512,512]{1,0:T(8,128)(2,1)S(1)}, u32[]{:S(2)}, u32[]{:S(2)}) collective-permute-start(bf16[512,512]{1,0:T(8,128)(2,1)S(1)} %collective-permute-done.1), channel_id=1, source_target_pairs={{0,1},{1,2},{2,3},{3,4},{4,5},{5,6},{6,7},{7,8},{8,9},{9,10},{10,1... | collective-permute-start | bytes 1572872 | tf_op jit(solution)/shard_map/ppermute | solution.py:21
  52.8 11.5 %collective-permute-start.3 = (bf16[512,512]{1,0:T(8,128)(2,1)S(1)}, bf16[512,512]{1,0:T(8,128)(2,1)S(1)}, u32[]{:S(2)}, u32[]{:S(2)}) collective-permute-start(bf16[512,512]{1,0:T(8,128)(2,1)S(1)} %collective-permute-done.2), channel_id=1, source_target_pairs={{0,1},{1,2},{2,3},{3,4},{4,5},{5,6},{6,7},{7,8},{8,9},{9,10},{10,1... | collective-permute-start | bytes 1572872 | tf_op jit(solution)/shard_map/ppermute | solution.py:21
  65.1 22.5 %collective-permute-start.4 = (bf16[512,512]{1,0:T(8,128)(2,1)S(1)}, bf16[512,512]{1,0:T(8,128)(2,1)S(1)}, u32[]{:S(2)}, u32[]{:S(2)}) collective-permute-start(bf16[512,512]{1,0:T(8,128)(2,1)S(1)} %collective-permute-done.3), channel_id=1, source_target_pairs={{0,1},{1,2},{2,3},{3,4},{4,5},{5,6},{6,7},{7,8},{8,9},{9,10},{10,1... | collective-permute-start | bytes 1572872 | tf_op jit(solution)/shard_map/ppermute | solution.py:21
  88.4 16.1 %collective-permute-start.5 = (bf16[512,512]{1,0:T(8,128)(2,1)S(1)}, bf16[512,512]{1,0:T(8,128)(2,1)S(1)}, u32[]{:S(2)}, u32[]{:S(2)}) collective-permute-start(bf16[512,512]{1,0:T(8,128)(2,1)S(1)} %collective-permute-done.4), channel_id=1, source_target_pairs={{0,1},{1,2},{2,3},{3,4},{4,5},{5,6},{6,7},{7,8},{8,9},{9,10},{10,1... | collective-permute-start | bytes 1572872 | tf_op jit(solution)/shard_map/ppermute | solution.py:21
  105.3 11.4 %collective-permute-start.6 = (bf16[512,512]{1,0:T(8,128)(2,1)S(1)}, bf16[512,512]{1,0:T(8,128)(2,1)S(1)}, u32[]{:S(2)}, u32[]{:S(2)}) collective-permute-start(bf16[512,512]{1,0:T(8,128)(2,1)S(1)} %collective-permute-done.5), channel_id=1, source_target_pairs={{0,1},{1,2},{2,3},{3,4},{4,5},{5,6},{6,7},{7,8},{8,9},{9,10},{10,1... | collective-permute-start | bytes 1572872 | tf_op jit(solution)/shard_map/ppermute | solution.py:21
  117.5 11.3 %collective-permute-start.7 = (bf16[512,512]{1,0:T(8,128)(2,1)S(1)}, bf16[512,512]{1,0:T(8,128)(2,1)S(1)}, u32[]{:S(2)}, u32[]{:S(2)}) collective-permute-start(bf16[512,512]{1,0:T(8,128)(2,1)S(1)} %collective-permute-done.6), channel_id=1, source_target_pairs={{0,1},{1,2},{2,3},{3,4},{4,5},{5,6},{6,7},{7,8},{8,9},{9,10},{10,1... | collective-permute-start | bytes 1572872 | tf_op jit(solution)/shard_map/ppermute | solution.py:21
  129.6 11.3 %collective-permute-start.8 = (bf16[512,512]{1,0:T(8,128)(2,1)S(1)}, bf16[512,512]{1,0:T(8,128)(2,1)S(1)}, u32[]{:S(2)}, u32[]{:S(2)}) collective-permute-start(bf16[512,512]{1,0:T(8,128)(2,1)S(1)} %collective-permute-done.7), channel_id=1, source_target_pairs={{0,1},{1,2},{2,3},{3,4},{4,5},{5,6},{6,7},{7,8},{8,9},{9,10},{10,1... | collective-permute-start | bytes 1572872 | tf_op jit(solution)/shard_map/ppermute | solution.py:21
  141.7 11.3 %collective-permute-start.9 = (bf16[512,512]{1,0:T(8,128)(2,1)S(1)}, bf16[512,512]{1,0:T(8,128)(2,1)S(1)}, u32[]{:S(2)}, u32[]{:S(2)}) collective-permute-start(bf16[512,512]{1,0:T(8,128)(2,1)S(1)} %collective-permute-done.8), channel_id=1, source_target_pairs={{0,1},{1,2},{2,3},{3,4},{4,5},{5,6},{6,7},{7,8},{8,9},{9,10},{10,1... | collective-permute-start | bytes 1572872 | tf_op jit(solution)/shard_map/ppermute | solution.py:21
  153.8 11.3 %collective-permute-start.10 = (bf16[512,512]{1,0:T(8,128)(2,1)S(1)}, bf16[512,512]{1,0:T(8,128)(2,1)S(1)}, u32[]{:S(2)}, u32[]{:S(2)}) collective-permute-start(bf16[512,512]{1,0:T(8,128)(2,1)S(1)} %collective-permute-done.9), channel_id=1, source_target_pairs={{0,1},{1,2},{2,3},{3,4},{4,5},{5,6},{6,7},{7,8},{8,9},{9,10},{10,1... | collective-permute-start | bytes 1572872 | tf_op jit(solution)/shard_map/ppermute | solution.py:21
  165.9 11.3 %collective-permute-start.11 = (bf16[512,512]{1,0:T(8,128)(2,1)S(1)}, bf16[512,512]{1,0:T(8,128)(2,1)S(1)}, u32[]{:S(2)}, u32[]{:S(2)}) collective-permute-start(bf16[512,512]{1,0:T(8,128)(2,1)S(1)} %collective-permute-done.10), channel_id=1, source_target_pairs={{0,1},{1,2},{2,3},{3,4},{4,5},{5,6},{6,7},{7,8},{8,9},{9,10},{10,1... | collective-permute-start | bytes 1572872 | tf_op jit(solution)/shard_map/ppermute | solution.py:21
  178.1 11.3 %collective-permute-start.12 = (bf16[512,512]{1,0:T(8,128)(2,1)S(1)}, bf16[512,512]{1,0:T(8,128)(2,1)S(1)}, u32[]{:S(2)}, u32[]{:S(2)}) collective-permute-start(bf16[512,512]{1,0:T(8,128)(2,1)S(1)} %collective-permute-done.11), channel_id=1, source_target_pairs={{0,1},{1,2},{2,3},{3,4},{4,5},{5,6},{6,7},{7,8},{8,9},{9,10},{10,1... | collective-permute-start | bytes 1572872 | tf_op jit(solution)/shard_map/ppermute | solution.py:21
  190.2 11.4 %collective-permute-start.13 = (bf16[512,512]{1,0:T(8,128)(2,1)S(1)}, bf16[512,512]{1,0:T(8,128)(2,1)}, u32[]{:S(2)}, u32[]{:S(2)}) collective-permute-start(bf16[512,512]{1,0:T(8,128)(2,1)S(1)} %collective-permute-done.12), channel_id=1, source_target_pairs={{0,1},{1,2},{2,3},{3,4},{4,5},{5,6},{6,7},{7,8},{8,9},{9,10},{10,1... | collective-permute-start | bytes 1572872 | tf_op jit(solution)/shard_map/ppermute | solution.py:21
  201.6 11.6 %collective-permute-start.14 = (bf16[512,512]{1,0:T(8,128)(2,1)}, bf16[512,512]{1,0:T(8,128)(2,1)}, u32[]{:S(2)}, u32[]{:S(2)}) collective-permute-start(bf16[512,512]{1,0:T(8,128)(2,1)} %collective-permute-done.13), channel_id=1, source_target_pairs={{0,1},{1,2},{2,3},{3,4},{4,5},{5,6},{6,7},{7,8},{8,9},{9,10},{10,1... | collective-permute-start | bytes 1572872 | tf_op jit(solution)/shard_map/ppermute | solution.py:21
  201.6 48.2 %copy-start.7 = (bf16[512,512]{1,0:T(8,128)(2,1)S(1)}, bf16[512,512]{1,0:T(8,128)(2,1)}, u32[]{:S(2)}) copy-start(bf16[512,512]{1,0:T(8,128)(2,1)} %copy-done.6) | copy-start | bytes 1572868
  201.6 49.0 %copy-start.5 = (bf16[512,512]{1,0:T(8,128)(2,1)S(1)}, bf16[512,512]{1,0:T(8,128)(2,1)}, u32[]{:S(2)}) copy-start(bf16[512,512]{1,0:T(8,128)(2,1)} %copy-done.4) | copy-start | bytes 1572868
  201.7 49.8 %copy-start.3 = (bf16[512,512]{1,0:T(8,128)(2,1)S(1)}, bf16[512,512]{1,0:T(8,128)(2,1)}, u32[]{:S(2)}) copy-start(bf16[512,512]{1,0:T(8,128)(2,1)} %copy-done.2) | copy-start | bytes 1572868
  286.9 44.8 %all-to-all-start.1 = ((bf16[16,512,128]{2,1,0:T(8,128)(2,1)}), bf16[16,512,128]{2,1,0:T(8,128)(2,1)S(1)}, u32[]{:S(2)}, u32[]{:S(2)}) async-start(bf16[16,512,128]{2,1,0:T(8,128)(2,1)} %bitcast.26), calls=%async_computation.1 | async-start | bytes 4194304 | tf_op jit(solution)/shard_map/all_to_all | solution.py:142
  334.5 52.4 %all-to-all-start = ((bf16[16,512,128]{2,1,0:T(8,128)(2,1)}), bf16[16,512,128]{2,1,0:T(8,128)(2,1)}, u32[]{:S(2)}, u32[]{:S(2)}) async-start(bf16[16,512,128]{2,1,0:T(8,128)(2,1)} %bitcast.4), calls=%async_computation | async-start | bytes 4194304 | tf_op jit(solution)/shard_map/all_to_all | solution.py:141
  345.7 126.0 %reduce-scatter.2.cloned.1.call-start = ((), (), s32[]{:S(2)}) async-start(), calls=%async_computation.4 | async-start | bytes 1114112 | tf_op jit(solution)/shard_map/reduce_scatter | solution.py:180
  (19 other events, 380.4 us)
Sparse Core Ops, SparseCore 0:
  19.2 88.5 all-gather.1
  406.4 65.2 reduce-scatter.1
